TPU v7x, 32 devices: a whole 2x2x4 slice. The times are simulated.
32 devices in a mesh: rep: 4 (over x, core), shard: 8 (over z, y).
Axes of the slice: x: 2, y: 2, z: 4, core: 2. Of those that a mesh axis runs over, the one named last changes fastest.
Arguments:
- block_input: float32 [32, 256, 768], P(('rep', 'shard')), may hold values from -6 to 6
- attn_gain: bfloat16 [768], P('shard'), may hold values from 0.099609375 to 1.8984375
- attn_shift: bfloat16 [768], P('shard'), may hold values from -3 to 3
- query_weight: bfloat16 [768, 768], P('shard'), may hold values from -4 to 4
- query_bias: bfloat16 [768], P('shard'), may hold values from -3 to 3
- key_weight: bfloat16 [768, 768], P('shard'), may hold values from -4 to 4
- value_weight: bfloat16 [768, 768], P('shard'), may hold values from -0.21875 to 0.21875
- value_bias: bfloat16 [768], P('shard'), may hold values from -0.3125 to 0.3125
- out_weight: bfloat16 [768, 768], P('shard'), may hold values from -3.5 to 3.5
- out_bias: bfloat16 [768], P('shard'), may hold values from -3 to 3
- mlp_gain: bfloat16 [768], P('shard'), may hold values from 0.099609375 to 1.8984375
- mlp_shift: bfloat16 [768], P('shard'), may hold values from -3 to 3
- hidden_weight: bfloat16 [768, 3072], P('shard'), may hold values from -0.21875 to 0.21875
- hidden_bias: bfloat16 [3072], P('shard'), may hold values from -3 to 3
- proj_weight: bfloat16 [3072, 768], P('shard'), may hold values from -0.109375 to 0.109375
- proj_bias: bfloat16 [768], P('shard'), may hold values from -3 to 3
- out_cotangent: float32 [32, 256, 768], P(('rep', 'shard')), may hold values from -6 to 6
Outputs:
- block_output: float32 [32, 256, 768], P(('rep', 'shard'))
- input_grad: float32 [32, 256, 768], P(('rep', 'shard'))
- attn_gain_grad: float32 [768], P('shard')
- attn_shift_grad: float32 [768], P('shard')
- query_weight_grad: float32 [768, 768], P('shard')
- query_bias_grad: float32 [768], P('shard')
- key_weight_grad: float32 [768, 768], P('shard')
- value_weight_grad: float32 [768, 768], P('shard')
- value_bias_grad: float32 [768], P('shard')
- out_weight_grad: float32 [768, 768], P('shard')
- out_bias_grad: float32 [768], P('shard')
- mlp_gain_grad: float32 [768], P('shard')
- mlp_shift_grad: float32 [768], P('shard')
- hidden_weight_grad: float32 [768, 3072], P('shard')
- hidden_bias_grad: float32 [3072], P('shard')
- proj_weight_grad: float32 [3072, 768], P('shard')
- proj_bias_grad: float32 [768], P('shard')
All inputs are finite; a program needn't handle non-finite values.
Results may differ from a plain program's by a relative error of at most 0.02.
The roundings to bfloat16 on the way count: a program that leaves them out, or rounds other values in their place, can miss the bound.
Values may be sent and summed in bfloat16 or wider, within the bound.
A program may use at most 128 MiB of HBM per device.

v0:
```python
import jax
import jax.numpy as jnp
from jax import lax
from jax.sharding import PartitionSpec as P

HD = 64
EPS = 1e-05
ROOT_HALF = 0.7071067811865476
INV_ROOT_TWO_PI = 0.3989422804014327


def layer_norm(tokens, norm_gain, norm_shift):
    average = jnp.mean(tokens, axis=-1, keepdims=True)
    centered = tokens - average
    inv_std = lax.rsqrt(jnp.mean(centered * centered, axis=-1, keepdims=True) + EPS)
    normed = centered * inv_std
    shaped = normed * norm_gain.astype(jnp.float32) + norm_shift.astype(jnp.float32)
    return (normed, inv_std, shaped.astype(jnp.bfloat16))


def norm_grad(upstream, normed, inv_std, norm_gain):
    scaled = upstream * norm_gain.astype(jnp.float32)
    inner = (
        scaled
        - jnp.mean(scaled, axis=-1, keepdims=True)
        - normed * jnp.mean(scaled * normed, axis=-1, keepdims=True)
    )
    return (inner * inv_std, jnp.sum(upstream * normed, axis=0), jnp.sum(upstream, axis=0))


def matmul(left, right):
    return jnp.dot(left, right, preferred_element_type=jnp.float32)


def times_transposed(left, right):
    return lax.dot_general(
        left, right, (((1,), (1,)), ((), ())), preferred_element_type=jnp.float32
    )


def token_sum(left, right):
    return lax.dot_general(
        left, right, (((0,), (0,)), ((), ())), preferred_element_type=jnp.float32
    )


def gelu_parts(before):
    normal_cdf = 0.5 * (1.0 + lax.erf(before * ROOT_HALF))
    return (
        before * normal_cdf,
        normal_cdf + before * INV_ROOT_TWO_PI * jnp.exp(-0.5 * before * before),
    )


def attend(query, keys, values):
    factor = query.shape[-1] ** (-0.5)
    scores = jnp.einsum("clhd,cmhd->chlm", query, keys, preferred_element_type=jnp.float32) * factor
    row_top = jnp.max(scores, axis=-1, keepdims=True)
    log_total = row_top + jnp.log(jnp.sum(jnp.exp(scores - row_top), axis=-1, keepdims=True))
    weights = jnp.exp(scores - log_total).astype(jnp.bfloat16)
    mixed = jnp.einsum(
        "chlm,cmhd->clhd", weights, values, preferred_element_type=jnp.float32
    ).astype(jnp.bfloat16)
    return (mixed, log_total)


def attend_grad(query, keys, values, mixed, log_total, grad_mixed):
    factor = query.shape[-1] ** (-0.5)
    scores = jnp.einsum("clhd,cmhd->chlm", query, keys, preferred_element_type=jnp.float32) * factor
    weights = jnp.exp(scores - log_total)
    weights_low = weights.astype(jnp.bfloat16)
    grad_values = jnp.einsum(
        "chlm,clhd->cmhd", weights_low, grad_mixed, preferred_element_type=jnp.float32
    )
    grad_weights = jnp.einsum(
        "clhd,cmhd->chlm", grad_mixed, values, preferred_element_type=jnp.float32
    )
    delta = jnp.sum(grad_mixed.astype(jnp.float32) * mixed.astype(jnp.float32), axis=-1)
    delta = jnp.transpose(delta, (0, 2, 1))[..., None]
    grad_scores = (weights * (grad_weights - delta)).astype(jnp.bfloat16)
    grad_query = (
        jnp.einsum("chlm,cmhd->clhd", grad_scores, keys, preferred_element_type=jnp.float32)
        * factor
    )
    grad_keys = (
        jnp.einsum("chlm,clhd->cmhd", grad_scores, query, preferred_element_type=jnp.float32)
        * factor
    )
    return (grad_query, grad_keys, grad_values)


def cut_columns(matrix, likes, flat=True):
    pieces = []
    start = 0
    for like in likes:
        width = like.shape[-1]
        piece = matrix[:, start : start + width]
        pieces.append(piece.reshape(-1) if flat else piece)
        start += width
    return tuple(pieces)


def on_device(
    block_input,
    attn_gain,
    attn_shift,
    query_weight,
    query_bias,
    key_weight,
    value_weight,
    value_bias,
    out_weight,
    out_bias,
    mlp_gain,
    mlp_shift,
    hidden_weight,
    hidden_bias,
    proj_weight,
    proj_bias,
    out_cotangent,
):
    clip_count, frame_count, model_width = block_input.shape
    head_count = model_width // HD
    token_count = clip_count * frame_count

    def split_heads(matrix):
        return matrix.reshape(clip_count, frame_count, head_count, HD)

    def join_heads(tensor):
        return tensor.reshape(token_count, model_width)

    residual = block_input.reshape(token_count, model_width)
    vectors = (
        attn_gain,
        attn_shift,
        query_bias,
        value_bias,
        out_bias,
        mlp_gain,
        mlp_shift,
        proj_bias,
        hidden_bias,
    )
    squares = (query_weight, key_weight, value_weight, out_weight, hidden_weight)
    vectors_all = lax.all_gather(jnp.concatenate(vectors), "shard", axis=0, tiled=False)
    squares_all = lax.all_gather(jnp.concatenate(squares, axis=1), "shard", axis=0, tiled=True)
    proj_all = lax.all_gather(proj_weight, "shard", axis=0, tiled=True)
    (
        attn_gain_all,
        attn_shift_all,
        query_bias_all,
        value_bias_all,
        out_bias_all,
        mlp_gain_all,
        mlp_shift_all,
        proj_bias_all,
        hidden_bias_all,
    ) = cut_columns(vectors_all, vectors)
    query_all, key_all, value_all, out_all, hidden_all = cut_columns(squares_all, squares, False)
    normed_one, inv_one, input_low = layer_norm(residual, attn_gain_all, attn_shift_all)
    query_low = (matmul(input_low, query_all) + query_bias_all.astype(jnp.float32)).astype(
        jnp.bfloat16
    )
    keys_low = matmul(input_low, key_all).astype(jnp.bfloat16)
    values_low = (matmul(input_low, value_all) + value_bias_all.astype(jnp.float32)).astype(
        jnp.bfloat16
    )
    mixed, log_total = attend(
        split_heads(query_low), split_heads(keys_low), split_heads(values_low)
    )
    mixed_rows = join_heads(mixed)
    middle = residual + matmul(mixed_rows, out_all) + out_bias_all.astype(jnp.float32)
    normed_two, inv_two, middle_low = layer_norm(middle, mlp_gain_all, mlp_shift_all)
    before_act = matmul(middle_low, hidden_all) + hidden_bias_all.astype(jnp.float32)
    activated, slope = gelu_parts(before_act)
    act_low = activated.astype(jnp.bfloat16)
    block_output = middle + matmul(act_low, proj_all) + proj_bias_all.astype(jnp.float32)
    upstream = out_cotangent.reshape(token_count, model_width)
    up_low = upstream.astype(jnp.bfloat16)
    proj_term = token_sum(act_low, up_low)
    proj_bias_term = jnp.sum(upstream, axis=0)
    grad_before = times_transposed(up_low, proj_all) * slope
    before_low = grad_before.astype(jnp.bfloat16)
    hidden_term = token_sum(middle_low, before_low)
    hidden_bias_term = jnp.sum(grad_before, axis=0)
    grad_normed_two = times_transposed(before_low, hidden_all)
    grad_middle_norm, mlp_gain_term, mlp_shift_term = norm_grad(
        grad_normed_two, normed_two, inv_two, mlp_gain_all
    )
    grad_middle = upstream + grad_middle_norm
    middle_grad_low = grad_middle.astype(jnp.bfloat16)
    out_term = token_sum(mixed_rows, middle_grad_low)
    out_bias_term = jnp.sum(grad_middle, axis=0)
    grad_mixed = times_transposed(middle_grad_low, out_all).astype(jnp.bfloat16)
    grad_query, grad_keys, grad_values = attend_grad(
        split_heads(query_low),
        split_heads(keys_low),
        split_heads(values_low),
        mixed,
        log_total,
        split_heads(grad_mixed),
    )
    grad_query = join_heads(grad_query)
    grad_keys = join_heads(grad_keys)
    grad_values = join_heads(grad_values)
    query_bias_term = jnp.sum(grad_query, axis=0)
    value_bias_term = jnp.sum(grad_values, axis=0)
    query_grad_low = grad_query.astype(jnp.bfloat16)
    key_grad_low = grad_keys.astype(jnp.bfloat16)
    value_grad_low = grad_values.astype(jnp.bfloat16)
    query_term = token_sum(input_low, query_grad_low)
    key_term = token_sum(input_low, key_grad_low)
    value_term = token_sum(input_low, value_grad_low)
    grad_normed_one = (
        times_transposed(query_grad_low, query_all)
        + times_transposed(key_grad_low, key_all)
        + times_transposed(value_grad_low, value_all)
    )
    grad_input_norm, attn_gain_term, attn_shift_term = norm_grad(
        grad_normed_one, normed_one, inv_one, attn_gain_all
    )
    input_grad = grad_middle + grad_input_norm
    shards = lax.axis_size("shard")
    vector_terms = jnp.concatenate(
        [
            term.reshape(shards, -1)
            for term in (
                attn_gain_term,
                attn_shift_term,
                query_bias_term,
                value_bias_term,
                out_bias_term,
                mlp_gain_term,
                mlp_shift_term,
                proj_bias_term,
                hidden_bias_term,
            )
        ],
        axis=1,
    )
    square_terms = jnp.concatenate(
        [
            term.astype(jnp.bfloat16)
            for term in (query_term, key_term, value_term, out_term, hidden_term)
        ],
        axis=1,
    )
    vector_owned = lax.psum(vector_terms, ("rep", "shard"))
    vector_owned = lax.dynamic_index_in_dim(
        vector_owned, lax.axis_index("shard"), 0, keepdims=False
    )
    square_owned = lax.psum_scatter(square_terms, "shard", scatter_dimension=0, tiled=True)
    proj_owned = lax.psum_scatter(
        proj_term.astype(jnp.bfloat16), "shard", scatter_dimension=0, tiled=True
    )
    square_owned = lax.psum(square_owned, "rep").astype(jnp.float32)
    proj_weight_grad = lax.psum(proj_owned, "rep").astype(jnp.float32)
    (
        attn_gain_grad,
        attn_shift_grad,
        query_bias_grad,
        value_bias_grad,
        out_bias_grad,
        mlp_gain_grad,
        mlp_shift_grad,
        proj_bias_grad,
        hidden_bias_grad,
    ) = cut_columns(vector_owned[None, :], vectors)
    query_weight_grad, key_weight_grad, value_weight_grad, out_weight_grad, hidden_weight_grad = (
        cut_columns(square_owned, squares, False)
    )
    return (
        block_output.reshape(clip_count, frame_count, model_width),
        input_grad.reshape(clip_count, frame_count, model_width),
        attn_gain_grad,
        attn_shift_grad,
        query_weight_grad,
        query_bias_grad,
        key_weight_grad,
        value_weight_grad,
        value_bias_grad,
        out_weight_grad,
        out_bias_grad,
        mlp_gain_grad,
        mlp_shift_grad,
        hidden_weight_grad,
        hidden_bias_grad,
        proj_weight_grad,
        proj_bias_grad,
    )


def solution(mesh):
    placed = (
        P(("rep", "shard"), None, None),
        P("shard"),
        P("shard"),
        P("shard", None),
        P("shard"),
        P("shard", None),
        P("shard", None),
        P("shard"),
        P("shard", None),
        P("shard"),
        P("shard"),
        P("shard"),
        P("shard", None),
        P("shard"),
        P("shard", None),
        P("shard"),
        P(("rep", "shard"), None, None),
    )
    return jax.shard_map(
        on_device,
        mesh=mesh,
        in_specs=placed,
        out_specs=(
            P(("rep", "shard"), None, None),
            P(("rep", "shard"), None, None),
            P("shard"),
            P("shard"),
            P("shard", None),
            P("shard"),
            P("shard", None),
            P("shard", None),
            P("shard"),
            P("shard", None),
            P("shard"),
            P("shard"),
            P("shard"),
            P("shard", None),
            P("shard"),
            P("shard", None),
            P("shard"),
        ),
        check_vma=False,
    )
```

profile of v0, /device:TPU:0, one launch (start us, length us, event | category | flops | bytes accessed | tf_op | source)
XLA Modules:
  0.0 555.6 jit_solution(15415747082169291236)
XLA Ops:
  14.3 33.4 %all-gather.1 = bf16[8,1,1152]{2,1,0:T(2,128)(2,1)S(1)} all-gather(bf16[1,1,1152]{2,1,0:T(2,128)(2,1)S(1)} %reshape.446), channel_id=2, replica_groups=mesh['rep'=4,'shard'=8] {'shard'}, dimensions={0}, use_global_device_ids=true | all-gather | bytes 20736 | tf_op jit(solution)/shard_map/all_gather | solution.py:145
  52.7 101.0 %all-gather.5.cloned.1.call-done = bf16[768,6144]{1,0:T(8,128)(2,1)} async-done(((bf16[96,6144]{1,0:T(8,128)(2,1)}), bf16[768,6144]{1,0:T(8,128)(2,1)}) %all-gather.5.cloned.1.call-update) | async-done | bytes 9437200 | tf_op jit(solution)/shard_map/all_gather | solution.py:146
  153.7 1.7 fusion.17
  156.4 1.7 convolution_convert_fusion.8
  158.3 1.9 fusion.16
  161.1 1.8 multiply_reduce_fusion
  166.7 3.3 multiply_convert_fusion.1
  171.3 3.7 fusion.47
  175.3 2.1 fusion.31
  177.4 56.0 %all-gather.7.cloned.1.call-done = bf16[3072,768]{1,0:T(8,128)(2,1)} async-done(((bf16[384,768]{1,0:T(8,128)(2,1)}), bf16[3072,768]{1,0:T(8,128)(2,1)}) %all-gather.7.cloned.1.call-update) | async-done | bytes 4718608 | tf_op jit(solution)/shard_map/all_gather | solution.py:147
  233.4 6.1 %fusion.45 = (f32[3072]{0:T(1024)}, bf16[256,3072]{1,0:T(8,128)(2,1)S(1)}) fusion(f32[256,3072]{1,0:T(8,128)} %get-tuple-element.58, bf16[3072,768]{1,0:T(8,128)(2,1)} %all-gather.7.cloned.1.call-done, f32[1,256,768]{2,1,0:T(8,128)} %param.33), kind=kOutput, calls=%fused_computation.119 | convolution fusion | flops 1216607232 | bytes 10235904 | tf_op jit(solution)/shard_map/dot_general | solution.py:36
  239.5 5.2 multiply_reduce_fusion.1
  246.5 2.5 convolution_convert_fusion.6
  249.1 1.9 copy.70
  251.0 2.0 copy.71
  253.0 2.7 convolution_convert_fusion.5
  255.7 2.4 copy.79
  258.1 2.4 fusion.42
  262.8 2.4 copy.78
  266.5 2.1 multiply_convert_fusion
  272.3 2.1 fusion.43
  276.6 1.7 copy.76
  283.1 3.8 fusion
  296.9 1.8 fusion.23
  298.7 1.8 convolution_add_fusion.1
  300.6 2.8 multiply_reduce_fusion.2
  305.7 40.4 %psum.21 = f32[8,1152]{1,0:T(8,128)S(1)} all-reduce(f32[8,1152]{1,0:T(8,128)S(1)} %concatenate.14), channel_id=1, replica_groups=mesh['rep'=4,'shard'=8] {'rep','shard'}, use_global_device_ids=true, to_apply=%region_20.0 | all-reduce | flops 9216 | bytes 73728 | tf_op jit(solution)/shard_map/psum | solution.py:248
  347.5 149.5 %reduce-scatter.3.cloned.1.call-done = bf16[96,6144]{1,0:T(8,128)(2,1)} async-done(((bf16[768,6144]{1,0:T(8,128)(2,1)}), bf16[96,6144]{1,0:T(8,128)(2,1)}) %reduce-scatter.3.cloned.1.call-update) | async-done | bytes 1179664 | tf_op jit(solution)/shard_map/reduce_scatter | solution.py:252
  498.4 1.8 add_bitcast_fusion
  500.2 4.6 fusion.15
  504.8 39.8 %all-reduce.3.cloned.1.call-done = (bf16[96,6144]{1,0:T(8,128)(2,1)}, bf16[384,768]{1,0:T(8,128)(2,1)}) async-done(((bf16[96,6144]{1,0:T(8,128)(2,1)}, bf16[384,768]{1,0:T(8,128)(2,1)}), (bf16[96,6144]{1,0:T(8,128)(2,1)}, bf16[384,768]{1,0:T(8,128)(2,1)})) %all-reduce.3.cloned.1.call-update) | async-done | bytes 1769488 | tf_op jit(solution)/shard_map/psum | solution.py:256
  544.6 2.3 slice.130
  (202 shorter events, 52.1 us)
Async XLA Ops:
  7.2 6.9 %copy-start.61 = (bf16[96]{0:T(256)(128)(2,1)S(1)}, bf16[96]{0:T(256)(128)(2,1)}, u32[]{:S(2)}) copy-start(bf16[96]{0:T(256)(128)(2,1)} %param.32) | copy-start | bytes 580
  7.2 6.9 %copy-start.53 = (bf16[384]{0:T(512)(128)(2,1)S(1)}, bf16[384]{0:T(512)(128)(2,1)}, u32[]{:S(2)}) copy-start(bf16[384]{0:T(512)(128)(2,1)} %param.30) | copy-start | bytes 2308
  7.2 6.9 %copy-start.60 = (bf16[96]{0:T(256)(128)(2,1)S(1)}, bf16[96]{0:T(256)(128)(2,1)}, u32[]{:S(2)}) copy-start(bf16[96]{0:T(256)(128)(2,1)} %param.28) | copy-start | bytes 580
  7.2 6.9 %copy-start.59 = (bf16[96]{0:T(256)(128)(2,1)S(1)}, bf16[96]{0:T(256)(128)(2,1)}, u32[]{:S(2)}) copy-start(bf16[96]{0:T(256)(128)(2,1)} %param.27) | copy-start | bytes 580
  7.2 6.9 %copy-start.58 = (bf16[96]{0:T(256)(128)(2,1)S(1)}, bf16[96]{0:T(256)(128)(2,1)}, u32[]{:S(2)}) copy-start(bf16[96]{0:T(256)(128)(2,1)} %param.26) | copy-start | bytes 580
  7.2 6.9 %copy-start.57 = (bf16[96]{0:T(256)(128)(2,1)S(1)}, bf16[96]{0:T(256)(128)(2,1)}, u32[]{:S(2)}) copy-start(bf16[96]{0:T(256)(128)(2,1)} %param.24) | copy-start | bytes 580
  7.3 6.9 %copy-start.56 = (bf16[96]{0:T(256)(128)(2,1)S(1)}, bf16[96]{0:T(256)(128)(2,1)}, u32[]{:S(2)}) copy-start(bf16[96]{0:T(256)(128)(2,1)} %param.21) | copy-start | bytes 580
  7.3 6.9 %copy-start.55 = (bf16[96]{0:T(256)(128)(2,1)S(1)}, bf16[96]{0:T(256)(128)(2,1)}, u32[]{:S(2)}) copy-start(bf16[96]{0:T(256)(128)(2,1)} %param.19) | copy-start | bytes 580
  7.3 6.9 %copy-start.54 = (bf16[96]{0:T(256)(128)(2,1)S(1)}, bf16[96]{0:T(256)(128)(2,1)}, u32[]{:S(2)}) copy-start(bf16[96]{0:T(256)(128)(2,1)} %param.18) | copy-start | bytes 580
  7.3 44.0 %copy-start = (f32[1,256,768]{2,1,0:T(8,128)S(1)}, f32[1,256,768]{2,1,0:T(8,128)}, u32[]{:S(2)}) copy-start(f32[1,256,768]{2,1,0:T(8,128)} %param.17) | copy-start | bytes 2359300
  7.3 146.4 %all-gather.5.cloned.1.call-start = ((), (), s32[]{:S(2)}) async-start(), calls=%async_computation.2 | async-start | bytes 10616832 | tf_op jit(solution)/shard_map/all_gather | solution.py:146
  13.3 220.2 %all-gather.7.cloned.1.call-start = ((), (), s32[]{:S(2)}) async-start(), calls=%async_computation.3 | async-start | bytes 5308416 | tf_op jit(solution)/shard_map/all_gather | solution.py:147
  14.0 333.5 %reduce-scatter.5.cloned.1.call-start = ((), (), s32[]{:S(2)}) async-start(), calls=%async_computation.5 | async-start | bytes 5308416 | tf_op jit(solution)/shard_map/reduce_scatter | solution.py:253
  49.7 108.4 %copy-start.33 = (f32[768]{0:T(1024)}, f32[768]{0:T(1024)S(1)}, u32[]{:S(2)}) copy-start(f32[768]{0:T(1024)S(1)} %reshape.435) | copy-start | bytes 9220
  50.4 107.7 %copy-start.35 = (f32[768]{0:T(1024)}, f32[768]{0:T(1024)S(1)}, u32[]{:S(2)}) copy-start(f32[768]{0:T(1024)S(1)} %reshape.436) | copy-start | bytes 9220
  158.3 4.7 copy-start.25
  166.7 4.6 copy-start.7
  175.0 322.0 %reduce-scatter.3.cloned.1.call-start = ((), (), s32[]{:S(2)}) async-start(), calls=%async_computation.4 | async-start | bytes 10616832 | tf_op jit(solution)/shard_map/reduce_scatter | solution.py:252
  233.4 6.1 %copy-start.11 = (f32[256,768]{1,0:T(8,128)S(1)}, f32[256,768]{1,0:T(8,128)}, u32[]{:S(2)}) copy-start(f32[256,768]{1,0:T(8,128)} %copy-done.10) | copy-start | bytes 2359300
  233.4 6.1 %copy-start.39 = (f32[768]{0:T(1024)S(1)}, f32[768]{0:T(1024)}, u32[]{:S(2)}) copy-start(f32[768]{0:T(1024)} %reshape.440) | copy-start | bytes 9220
  233.4 6.1 %copy-start.45 = (f32[256]{0:T(256)S(1)}, f32[256]{0:T(256)}, u32[]{:S(2)}) copy-start(f32[256]{0:T(256)} %copy-done.44) | copy-start | bytes 3076
  233.4 6.1 %copy-start.48 = (f32[256]{0:T(256)S(1)}, f32[256]{0:T(256)}, u32[]{:S(2)}) copy-start(f32[256]{0:T(256)} %copy-done.47) | copy-start | bytes 3076
  239.5 5.2 copy-start.62
  239.5 5.2 copy-start.8
  286.9 10.0 %copy-start.24 = (bf16[1,256,12,64]{1,3,2,0:T(8,128)(2,1)S(1)}, bf16[1,256,12,64]{1,3,2,0:T(8,128)(2,1)}, u32[]{:S(2)}) copy-start(bf16[1,256,12,64]{1,3,2,0:T(8,128)(2,1)} %copy-done.23) | copy-start | bytes 1179652
  287.0 11.8 %copy-start.22 = (bf16[12,64,256]{2,1,0:T(8,128)(2,1)S(1)}, bf16[12,64,256]{2,1,0:T(8,128)(2,1)}, u32[]{:S(2)}) copy-start(bf16[12,64,256]{2,1,0:T(8,128)(2,1)} %copy-done.21) | copy-start | bytes 1179652
  287.0 257.6 %all-reduce.3.cloned.1.call-start = ((), (), s32[]{:S(2)}) async-start(), calls=%async_computation.6 | async-start | bytes 3538944 | tf_op jit(solution)/shard_map/psum | solution.py:256
  288.1 12.5 %copy-start.2 = (f32[1,256,768]{2,1,0:T(8,128)S(1)}, f32[1,256,768]{2,1,0:T(8,128)}, u32[]{:S(2)}) copy-start(f32[1,256,768]{2,1,0:T(8,128)} %param.17) | copy-start | bytes 2359300
  288.1 12.5 %copy-start.30 = (bf16[1,256,12,64]{1,3,2,0:T(8,128)(2,1)S(1)}, bf16[1,256,12,64]{1,3,2,0:T(8,128)(2,1)}, u32[]{:S(2)}) copy-start(bf16[1,256,12,64]{1,3,2,0:T(8,128)(2,1)} %copy-done.29) | copy-start | bytes 1179652
  288.1 12.5 %copy-start.34 = (f32[768]{0:T(1024)S(1)}, f32[768]{0:T(1024)}, u32[]{:S(2)}) copy-start(f32[768]{0:T(1024)} %copy-done.33) | copy-start | bytes 9220
  300.6 197.8 %copy-start.6 = (f32[256,768]{1,0:T(8,128)S(1)}, f32[256,768]{1,0:T(8,128)}, u32[]{:S(2)}) copy-start(f32[256,768]{1,0:T(8,128)} %copy-done.5) | copy-start | bytes 2359300
  303.4 196.8 %copy-start.52 = (f32[768]{0:T(1024)S(1)}, f32[768]{0:T(1024)}, u32[]{:S(2)}) copy-start(f32[768]{0:T(1024)} %reshape.443) | copy-start | bytes 9220
  (37 other events, 100.6 us)
Sparse Core Ops, SparseCore 0:
  13.4 140.2 all-gather.4
  155.9 77.5 all-gather.6
  237.1 94.7 reduce-scatter.4
  335.3 161.7 reduce-scatter.2
  499.4 45.1 all-reduce.2
where the time goes:
time: 557 us; the launch traced here: 556 us
  waiting for transfers between devices  347 us (62%)
  blocking collectives  73.9 us (13%)
  matrix products  57.4 us (10%)
  local copies, waits for them, and re-layouts  51.4 us (9%)
  between operations  14.5 us (3%)
  other arithmetic  10.7 us (2%)
    reduce_scatter x1, waiting for transfers between devices, on_device(): lax.psum_scatter(square_terms, 'shard', scatter_dimension=0, tiled=True)  150 us
    all_gather x1, waiting for transfers between devices, on_device(): lax.all_gather(jnp.concatenate(squares, axis=1), 'shard', axis=0, tiled=T...  101 us
    all_gather x1, waiting for transfers between devices, on_device(): proj_all = lax.all_gather(proj_weight, 'shard', axis=0, tiled=True)  56 us
    psum x1, blocking collectives, on_device(): vector_owned = lax.psum(vector_terms, ('rep', 'shard'))  40.4 us
    psum x1, waiting for transfers between devices, on_device(): square_owned = lax.psum(square_owned, 'rep').astype(jnp.float32)  39.8 us
    all_gather x1, blocking collectives, on_device(): lax.all_gather(jnp.concatenate(vectors), 'shard', axis=0, tiled=False)  33.4 us
    dot_general x6, matrix products, times_transposed(): lax.dot_general(left, right, (((1,), (1,)), ((), ())), preferred_element_...  20.2 us
    unnamed x138, local copies, waits for them, and re-layouts  17.6 us
  transfers between devices with their start and end apart: 5, of which 4 were waited for; matrix products, arithmetic and copies ran while one was open for 18% of the time, Pallas kernels for 0%

commit v1 on v0

--- a/solution.py
+++ b/solution.py
@@ -245,7 +245,7 @@
         ],
         axis=1,
     )
-    vector_owned = lax.psum(vector_terms, ("rep", "shard"))
+    vector_owned = lax.psum(lax.psum(vector_terms, "rep"), "shard")
     vector_owned = lax.dynamic_index_in_dim(
         vector_owned, lax.axis_index("shard"), 0, keepdims=False
     )

time: 557 us -> 557 us (level)
  waiting for transfers between devices: 347 us -> 339 us
  blocking collectives: 73.9 us -> 81.7 us
    reduce_scatter x1, waiting for transfers between devices: 150 us -> 142 us  [on_device(): lax.psum_scatter(square_terms, 'shard', scatter_dimension=0, tiled=True)]
    psum x1 -> x2, blocking collectives: 40.4 us -> 48.2 us  [on_device(): vector_owned = lax.psum(lax.psum(vector_terms, 'rep'), 'shard')]
where the time goes in v1:
time: 557 us; the launch traced here: 556 us
  waiting for transfers between devices  339 us (61%)
  blocking collectives  81.7 us (15%)
  matrix products  57.3 us (10%)
  local copies, waits for them, and re-layouts  51.6 us (9%)
  between operations  14.5 us (3%)
  other arithmetic  10.8 us (2%)
    reduce_scatter x1, waiting for transfers between devices, on_device(): lax.psum_scatter(square_terms, 'shard', scatter_dimension=0, tiled=True)  142 us
    all_gather x1, waiting for transfers between devices, on_device(): lax.all_gather(jnp.concatenate(squares, axis=1), 'shard', axis=0, tiled=T...  101 us
    all_gather x1, waiting for transfers between devices, on_device(): proj_all = lax.all_gather(proj_weight, 'shard', axis=0, tiled=True)  56 us
    psum x2, blocking collectives, on_device(): vector_owned = lax.psum(lax.psum(vector_terms, 'rep'), 'shard')  48.2 us
    psum x1, waiting for transfers between devices, on_device(): square_owned = lax.psum(square_owned, 'rep').astype(jnp.float32)  39.8 us
    all_gather x1, blocking collectives, on_device(): lax.all_gather(jnp.concatenate(vectors), 'shard', axis=0, tiled=False)  33.4 us
    dot_general x6, matrix products, times_transposed(): lax.dot_general(left, right, (((1,), (1,)), ((), ())), preferred_element_...  20.2 us
    unnamed x138, local copies, waits for them, and re-layouts  17.9 us
  transfers between devices with their start and end apart: 5, of which 4 were waited for; matrix products, arithmetic and copies ran while one was open for 18% of the time, Pallas kernels for 0%

profile of v1, /device:TPU:0, one launch (start us, length us, event | category | flops | bytes accessed | tf_op | source)
XLA Modules:
  0.0 555.5 jit_solution(8204235051085811143)
XLA Ops:
  14.3 33.4 %all-gather.1 = bf16[8,1,1152]{2,1,0:T(2,128)(2,1)S(1)} all-gather(bf16[1,1,1152]{2,1,0:T(2,128)(2,1)S(1)} %reshape.446), channel_id=2, replica_groups=mesh['rep'=4,'shard'=8] {'shard'}, dimensions={0}, use_global_device_ids=true | all-gather | bytes 20736 | tf_op jit(solution)/shard_map/all_gather | solution.py:145
  52.8 100.9 %all-gather.5.cloned.1.call-done = bf16[768,6144]{1,0:T(8,128)(2,1)} async-done(((bf16[96,6144]{1,0:T(8,128)(2,1)}), bf16[768,6144]{1,0:T(8,128)(2,1)}) %all-gather.5.cloned.1.call-update) | async-done | bytes 9437200 | tf_op jit(solution)/shard_map/all_gather | solution.py:146
  153.7 1.7 fusion.17
  156.4 1.7 convolution_convert_fusion.8
  158.3 1.9 fusion.16
  161.1 1.8 multiply_reduce_fusion
  166.7 3.4 multiply_convert_fusion.1
  171.4 3.7 fusion.47
  175.3 2.1 fusion.31
  177.4 56.0 %all-gather.7.cloned.1.call-done = bf16[3072,768]{1,0:T(8,128)(2,1)} async-done(((bf16[384,768]{1,0:T(8,128)(2,1)}), bf16[3072,768]{1,0:T(8,128)(2,1)}) %all-gather.7.cloned.1.call-update) | async-done | bytes 4718608 | tf_op jit(solution)/shard_map/all_gather | solution.py:147
  233.4 6.1 %fusion.45 = (f32[3072]{0:T(1024)}, bf16[256,3072]{1,0:T(8,128)(2,1)S(1)}) fusion(f32[256,3072]{1,0:T(8,128)} %get-tuple-element.58, bf16[3072,768]{1,0:T(8,128)(2,1)} %all-gather.7.cloned.1.call-done, f32[1,256,768]{2,1,0:T(8,128)} %param.33), kind=kOutput, calls=%fused_computation.119 | convolution fusion | flops 1216607232 | bytes 10235904 | tf_op jit(solution)/shard_map/dot_general | solution.py:36
  239.5 5.2 multiply_reduce_fusion.1
  246.6 2.5 convolution_convert_fusion.6
  249.1 1.9 copy.70
  251.0 2.0 copy.71
  253.1 2.7 convolution_convert_fusion.5
  255.7 2.4 copy.79
  258.1 2.4 fusion.42
  262.8 2.4 copy.78
  266.5 2.1 multiply_convert_fusion
  272.3 2.1 fusion.43
  283.3 3.8 fusion
  297.0 1.8 fusion.23
  298.8 1.8 convolution_add_fusion.1
  300.7 2.8 multiply_reduce_fusion.2
  305.8 10.9 %psum.28 = f32[8,1152]{1,0:T(8,128)S(1)} all-reduce(f32[8,1152]{1,0:T(8,128)S(1)} %concatenate.14), channel_id=1, replica_groups=mesh['rep'=4,'shard'=8] {'rep'}, use_global_device_ids=true, to_apply=%region_20.0 | all-reduce | flops 9216 | bytes 73728 | tf_op jit(solution)/shard_map/psum | solution.py:248
  316.7 37.4 %psum.29 = f32[8,1152]{1,0:T(8,128)S(1)} all-reduce(f32[8,1152]{1,0:T(8,128)S(1)} %psum.28), channel_id=1, replica_groups=mesh['rep'=4,'shard'=8] {'shard'}, use_global_device_ids=true, to_apply=%region_21.0 | all-reduce | flops 9216 | bytes 73728 | tf_op jit(solution)/shard_map/psum | solution.py:248
  355.4 141.6 %reduce-scatter.3.cloned.1.call-done = bf16[96,6144]{1,0:T(8,128)(2,1)} async-done(((bf16[768,6144]{1,0:T(8,128)(2,1)}), bf16[96,6144]{1,0:T(8,128)(2,1)}) %reduce-scatter.3.cloned.1.call-update) | async-done | bytes 1179664 | tf_op jit(solution)/shard_map/reduce_scatter | solution.py:252
  498.3 1.8 add_bitcast_fusion
  500.2 4.6 fusion.15
  504.8 39.8 %all-reduce.3.cloned.1.call-done = (bf16[96,6144]{1,0:T(8,128)(2,1)}, bf16[384,768]{1,0:T(8,128)(2,1)}) async-done(((bf16[96,6144]{1,0:T(8,128)(2,1)}, bf16[384,768]{1,0:T(8,128)(2,1)}), (bf16[96,6144]{1,0:T(8,128)(2,1)}, bf16[384,768]{1,0:T(8,128)(2,1)})) %all-reduce.3.cloned.1.call-update) | async-done | bytes 1769488 | tf_op jit(solution)/shard_map/psum | solution.py:256
  544.6 2.3 slice.130
  (203 shorter events, 54.0 us)
Async XLA Ops:
  7.2 6.9 %copy-start.61 = (bf16[96]{0:T(256)(128)(2,1)S(1)}, bf16[96]{0:T(256)(128)(2,1)}, u32[]{:S(2)}) copy-start(bf16[96]{0:T(256)(128)(2,1)} %param.32) | copy-start | bytes 580
  7.2 6.9 %copy-start.53 = (bf16[384]{0:T(512)(128)(2,1)S(1)}, bf16[384]{0:T(512)(128)(2,1)}, u32[]{:S(2)}) copy-start(bf16[384]{0:T(512)(128)(2,1)} %param.30) | copy-start | bytes 2308
  7.2 6.9 %copy-start.60 = (bf16[96]{0:T(256)(128)(2,1)S(1)}, bf16[96]{0:T(256)(128)(2,1)}, u32[]{:S(2)}) copy-start(bf16[96]{0:T(256)(128)(2,1)} %param.28) | copy-start | bytes 580
  7.2 6.9 %copy-start.59 = (bf16[96]{0:T(256)(128)(2,1)S(1)}, bf16[96]{0:T(256)(128)(2,1)}, u32[]{:S(2)}) copy-start(bf16[96]{0:T(256)(128)(2,1)} %param.27) | copy-start | bytes 580
  7.2 6.9 %copy-start.58 = (bf16[96]{0:T(256)(128)(2,1)S(1)}, bf16[96]{0:T(256)(128)(2,1)}, u32[]{:S(2)}) copy-start(bf16[96]{0:T(256)(128)(2,1)} %param.26) | copy-start | bytes 580
  7.2 6.9 %copy-start.57 = (bf16[96]{0:T(256)(128)(2,1)S(1)}, bf16[96]{0:T(256)(128)(2,1)}, u32[]{:S(2)}) copy-start(bf16[96]{0:T(256)(128)(2,1)} %param.24) | copy-start | bytes 580
  7.3 6.9 %copy-start.56 = (bf16[96]{0:T(256)(128)(2,1)S(1)}, bf16[96]{0:T(256)(128)(2,1)}, u32[]{:S(2)}) copy-start(bf16[96]{0:T(256)(128)(2,1)} %param.21) | copy-start | bytes 580
  7.3 6.9 %copy-start.55 = (bf16[96]{0:T(256)(128)(2,1)S(1)}, bf16[96]{0:T(256)(128)(2,1)}, u32[]{:S(2)}) copy-start(bf16[96]{0:T(256)(128)(2,1)} %param.19) | copy-start | bytes 580
  7.3 6.9 %copy-start.54 = (bf16[96]{0:T(256)(128)(2,1)S(1)}, bf16[96]{0:T(256)(128)(2,1)}, u32[]{:S(2)}) copy-start(bf16[96]{0:T(256)(128)(2,1)} %param.18) | copy-start | bytes 580
  7.3 44.0 %copy-start = (f32[1,256,768]{2,1,0:T(8,128)S(1)}, f32[1,256,768]{2,1,0:T(8,128)}, u32[]{:S(2)}) copy-start(f32[1,256,768]{2,1,0:T(8,128)} %param.17) | copy-start | bytes 2359300
  7.3 146.4 %all-gather.5.cloned.1.call-start = ((), (), s32[]{:S(2)}) async-start(), calls=%async_computation.2 | async-start | bytes 10616832 | tf_op jit(solution)/shard_map/all_gather | solution.py:146
  13.3 220.2 %all-gather.7.cloned.1.call-start = ((), (), s32[]{:S(2)}) async-start(), calls=%async_computation.3 | async-start | bytes 5308416 | tf_op jit(solution)/shard_map/all_gather | solution.py:147
  14.0 341.4 %reduce-scatter.5.cloned.1.call-start = ((), (), s32[]{:S(2)}) async-start(), calls=%async_computation.5 | async-start | bytes 5308416 | tf_op jit(solution)/shard_map/reduce_scatter | solution.py:253
  49.7 108.4 %copy-start.33 = (f32[768]{0:T(1024)}, f32[768]{0:T(1024)S(1)}, u32[]{:S(2)}) copy-start(f32[768]{0:T(1024)S(1)} %reshape.435) | copy-start | bytes 9220
  50.4 107.7 %copy-start.35 = (f32[768]{0:T(1024)}, f32[768]{0:T(1024)S(1)}, u32[]{:S(2)}) copy-start(f32[768]{0:T(1024)S(1)} %reshape.436) | copy-start | bytes 9220
  158.3 4.7 copy-start.25
  166.7 4.6 copy-start.7
  175.1 321.9 %reduce-scatter.3.cloned.1.call-start = ((), (), s32[]{:S(2)}) async-start(), calls=%async_computation.4 | async-start | bytes 10616832 | tf_op jit(solution)/shard_map/reduce_scatter | solution.py:252
  233.4 6.1 %copy-start.11 = (f32[256,768]{1,0:T(8,128)S(1)}, f32[256,768]{1,0:T(8,128)}, u32[]{:S(2)}) copy-start(f32[256,768]{1,0:T(8,128)} %copy-done.10) | copy-start | bytes 2359300
  233.4 6.1 %copy-start.39 = (f32[768]{0:T(1024)S(1)}, f32[768]{0:T(1024)}, u32[]{:S(2)}) copy-start(f32[768]{0:T(1024)} %reshape.440) | copy-start | bytes 9220
  233.4 6.1 %copy-start.45 = (f32[256]{0:T(256)S(1)}, f32[256]{0:T(256)}, u32[]{:S(2)}) copy-start(f32[256]{0:T(256)} %copy-done.44) | copy-start | bytes 3076
  233.4 6.1 %copy-start.48 = (f32[256]{0:T(256)S(1)}, f32[256]{0:T(256)}, u32[]{:S(2)}) copy-start(f32[256]{0:T(256)} %copy-done.47) | copy-start | bytes 3076
  239.5 5.2 copy-start.62
  239.5 5.2 copy-start.8
  287.1 10.0 %copy-start.24 = (bf16[1,256,12,64]{1,3,2,0:T(8,128)(2,1)S(1)}, bf16[1,256,12,64]{1,3,2,0:T(8,128)(2,1)}, u32[]{:S(2)}) copy-start(bf16[1,256,12,64]{1,3,2,0:T(8,128)(2,1)} %copy-done.23) | copy-start | bytes 1179652
  287.1 11.7 %copy-start.22 = (bf16[12,64,256]{2,1,0:T(8,128)(2,1)S(1)}, bf16[12,64,256]{2,1,0:T(8,128)(2,1)}, u32[]{:S(2)}) copy-start(bf16[12,64,256]{2,1,0:T(8,128)(2,1)} %copy-done.21) | copy-start | bytes 1179652
  287.1 257.5 %all-reduce.3.cloned.1.call-start = ((), (), s32[]{:S(2)}) async-start(), calls=%async_computation.6 | async-start | bytes 3538944 | tf_op jit(solution)/shard_map/psum | solution.py:256
  288.2 12.5 %copy-start.2 = (f32[1,256,768]{2,1,0:T(8,128)S(1)}, f32[1,256,768]{2,1,0:T(8,128)}, u32[]{:S(2)}) copy-start(f32[1,256,768]{2,1,0:T(8,128)} %param.17) | copy-start | bytes 2359300
  288.2 12.5 %copy-start.30 = (bf16[1,256,12,64]{1,3,2,0:T(8,128)(2,1)S(1)}, bf16[1,256,12,64]{1,3,2,0:T(8,128)(2,1)}, u32[]{:S(2)}) copy-start(bf16[1,256,12,64]{1,3,2,0:T(8,128)(2,1)} %copy-done.29) | copy-start | bytes 1179652
  288.2 12.5 %copy-start.34 = (f32[768]{0:T(1024)S(1)}, f32[768]{0:T(1024)}, u32[]{:S(2)}) copy-start(f32[768]{0:T(1024)} %copy-done.33) | copy-start | bytes 9220
  300.7 197.7 %copy-start.6 = (f32[256,768]{1,0:T(8,128)S(1)}, f32[256,768]{1,0:T(8,128)}, u32[]{:S(2)}) copy-start(f32[256,768]{1,0:T(8,128)} %copy-done.5) | copy-start | bytes 2359300
  303.4 196.7 %copy-start.52 = (f32[768]{0:T(1024)S(1)}, f32[768]{0:T(1024)}, u32[]{:S(2)}) copy-start(f32[768]{0:T(1024)} %reshape.443) | copy-start | bytes 9220
  (37 other events, 101.7 us)
Sparse Core Ops, SparseCore 0:
  13.4 140.2 all-gather.4
  155.9 77.5 all-gather.6
  237.1 94.6 reduce-scatter.4
  335.2 161.7 reduce-scatter.2
  499.4 45.1 all-reduce.2
